TPU v7x, 32 devices: a whole 2x2x4 slice. The times are simulated.
32 devices in a mesh: dp: 8 (over z, x), seq: 4 (over y, core).
Axes of the slice: x: 2, y: 2, z: 4, core: 2. Of those that a mesh axis runs over, the one named last changes fastest.
Arguments:
- tokens: bfloat16 [16384, 1024], P(('dp', 'seq')), may hold values from -6 to 6
- time_embed: bfloat16 [32, 1024], P(('dp', 'seq')), may hold values from -6 to 6
- lengths: int32 [32], P('dp'), may hold values from 0 to 475, as said below
- cotangent: bfloat16 [16384, 1024], P(('dp', 'seq')), may hold values from -6 to 6
- w_query: bfloat16 [1024, 1024], P('seq'), may hold values from -0.1875 to 0.1875
- w_key: bfloat16 [1024, 1024], P('seq'), may hold values from -0.1875 to 0.1875
- w_value: bfloat16 [1024, 1024], P('seq'), may hold values from -0.1875 to 0.1875
- w_out: bfloat16 [1024, 1024], P('seq'), may hold values from -0.75 to 0.75
- w_time: bfloat16 [1024, 1024], P('seq'), may hold values from -0.1875 to 0.1875
- w_in: bfloat16 [4096, 1024], P('seq'), may hold values from -0.1875 to 0.1875
- w_down: bfloat16 [4096, 1024], P('seq'), may hold values from -0.09375 to 0.09375
- b_query: bfloat16 [1024], replicated, may hold values from -3 to 3
- b_value: bfloat16 [1024], replicated, may hold values from -3 to 3
- b_out: bfloat16 [1024], replicated, may hold values from -3 to 3
- b_time: bfloat16 [1024], replicated, may hold values from -3 to 3
- b_in: bfloat16 [4096], replicated, may hold values from -3 to 3
- b_down: bfloat16 [1024], replicated, may hold values from -2 to 2
- gain_one: bfloat16 [1024], replicated, may hold values from 0.25 to 1.75
- shift_one: bfloat16 [1024], replicated, may hold values from -2 to 2
- gain_two: bfloat16 [1024], replicated, may hold values from 0.25 to 1.75
- shift_two: bfloat16 [1024], replicated, may hold values from -2 to 2
Outputs:
- layer_out: bfloat16 [16384, 1024], P(('dp', 'seq'))
- grad_tokens: bfloat16 [16384, 1024], P(('dp', 'seq'))
- grad_w_query: float32 [1024, 1024], P('seq')
- grad_w_key: float32 [1024, 1024], P('seq')
- grad_w_value: float32 [1024, 1024], P('seq')
- grad_w_out: float32 [1024, 1024], P('seq')
- grad_w_time: float32 [1024, 1024], P('seq')
- grad_w_in: float32 [4096, 1024], P('seq')
- grad_w_down: float32 [4096, 1024], P('seq')
- grad_b_query: float32 [1024], replicated
- grad_b_value: float32 [1024], replicated
- grad_b_out: float32 [1024], replicated
- grad_b_time: float32 [1024], replicated
- grad_b_in: float32 [4096], replicated
- grad_b_down: float32 [1024], replicated
- grad_gain_one: float32 [1024], replicated
- grad_shift_one: float32 [1024], replicated
- grad_gain_two: float32 [1024], replicated
- grad_shift_two: float32 [1024], replicated
Inputs may be any that keep to these rules, and one draw needn't show every extreme that they name: Item i's valid slots are its first lengths[i] + 25; every draw has an item of length 475 and one of length 0.
All inputs are finite; a program needn't handle non-finite values.
Results may differ from a plain program's by a relative error of at most 0.02.
Values may be sent and summed in bfloat16 or wider, within the bound.
A program may use at most 256 MiB of HBM per device.

v0:
```python
import jax
import jax.numpy as jnp
from jax import lax
from jax.sharding import PartitionSpec as P

HEAD_DIM = 64
BLOCK = 25
norm_eps = 1e-05
neg_large = -1e30


def layer_norm(values, gain, shift):
    center = values - jnp.mean(values, axis=-1, keepdims=True)
    spread = lax.rsqrt(jnp.mean(center * center, axis=-1, keepdims=True) + norm_eps)
    return center * spread * gain + shift


def exact_gelu(values):
    return jax.nn.gelu(values, approximate=False)


def split_heads(rows):
    return rows.reshape(rows.shape[0], rows.shape[1] // HEAD_DIM, HEAD_DIM)


def item_scores(item_block, key_valid):
    queries = split_heads(item_block[:, 0])
    key_heads = split_heads(item_block[:, 1])
    value_heads = split_heads(item_block[:, 2])
    scores = jnp.einsum(
        "qhd,khd->hqk", queries, key_heads, preferred_element_type=jnp.float32
    ) * HEAD_DIM ** (-0.5)
    masked = jnp.where(key_valid[None, None, :], scores, neg_large)
    return (queries, key_heads, value_heads, masked)


def attend_forward(packed):
    item_block, key_valid = packed
    queries, key_heads, value_heads, masked = item_scores(item_block, key_valid)
    row_max = jnp.max(masked, axis=-1, keepdims=True)
    exp_scores = jnp.exp(masked - row_max)
    row_total = jnp.sum(exp_scores, axis=-1, keepdims=True)
    soft_weights = (exp_scores / row_total).astype(jnp.bfloat16)
    mixed_heads = jnp.einsum(
        "hqk,khd->qhd", soft_weights, value_heads, preferred_element_type=jnp.float32
    )
    log_total = row_max[:, :, 0] + jnp.log(row_total[:, :, 0])
    return (mixed_heads.reshape(item_block.shape[0], -1).astype(jnp.bfloat16), log_total)


def attend_backward(packed):
    item_block, key_valid, log_total, grad_block = packed
    queries, key_heads, value_heads, masked = item_scores(item_block, key_valid)
    soft_weights = jnp.exp(masked - log_total[:, :, None])
    grad_heads = split_heads(grad_block)
    grad_value = jnp.einsum(
        "hqk,qhd->khd",
        soft_weights.astype(jnp.bfloat16),
        grad_heads,
        preferred_element_type=jnp.float32,
    )
    grad_soft = jnp.einsum(
        "qhd,khd->hqk", grad_heads, value_heads, preferred_element_type=jnp.float32
    )
    grad_scores = soft_weights * (
        grad_soft - jnp.sum(soft_weights * grad_soft, axis=-1, keepdims=True)
    )
    scores_low = grad_scores.astype(jnp.bfloat16)
    score_scale = HEAD_DIM ** (-0.5)
    grad_query = (
        jnp.einsum("hqk,khd->qhd", scores_low, key_heads, preferred_element_type=jnp.float32)
        * score_scale
    )
    grad_key = (
        jnp.einsum("hqk,qhd->khd", scores_low, queries, preferred_element_type=jnp.float32)
        * score_scale
    )
    slot_count = item_block.shape[0]
    return jnp.stack(
        [
            grad_query.reshape(slot_count, -1),
            grad_key.reshape(slot_count, -1),
            grad_value.reshape(slot_count, -1),
        ],
        axis=1,
    ).astype(jnp.bfloat16)


def local(
    tokens,
    time_embed,
    lengths,
    cotangent,
    w_query,
    w_key,
    w_value,
    w_out,
    w_time,
    w_in,
    w_down,
    b_query,
    b_value,
    b_out,
    b_time,
    b_in,
    b_down,
    gain_one,
    shift_one,
    gain_two,
    shift_two,
):
    seq_rank = lax.axis_index("seq")
    item_count = time_embed.shape[0]
    token_count = tokens.shape[0]
    slot_count = token_count // item_count
    model_width = tokens.shape[1]
    full_query, full_key, full_value, full_out, full_time, full_in, full_down = (
        lax.all_gather(w_query, "seq", axis=0, tiled=True),
        lax.all_gather(w_key, "seq", axis=0, tiled=True),
        lax.all_gather(w_value, "seq", axis=0, tiled=True),
        lax.all_gather(w_out, "seq", axis=0, tiled=True),
        lax.all_gather(w_time, "seq", axis=0, tiled=True),
        lax.all_gather(w_in, "seq", axis=0, tiled=True),
        lax.all_gather(w_down, "seq", axis=0, tiled=True),
    )
    bias_query = b_query.astype(jnp.float32)
    bias_value = b_value.astype(jnp.float32)
    bias_out = b_out.astype(jnp.float32)
    bias_time = b_time.astype(jnp.float32)
    bias_in = b_in.astype(jnp.float32)
    bias_down = b_down.astype(jnp.float32)
    gain_first = gain_one.astype(jnp.float32)
    shift_first = shift_one.astype(jnp.float32)
    gain_last = gain_two.astype(jnp.float32)
    shift_last = shift_two.astype(jnp.float32)
    slot_index = lax.broadcasted_iota(jnp.int32, (lengths.shape[0], slot_count), 1)
    group_valid = slot_index < lengths[:, None] + BLOCK
    own_valid = lax.dynamic_slice_in_dim(group_valid, seq_rank * item_count, item_count, 0)
    row_keep = own_valid.reshape(token_count, 1).astype(jnp.float32)
    time_proj = jnp.dot(time_embed, full_time, preferred_element_type=jnp.float32) + bias_time
    resid = (tokens.reshape(item_count, slot_count, model_width) + time_proj[:, None, :]).reshape(
        token_count, model_width
    )
    resid_low = resid.astype(jnp.bfloat16)
    query_rows = (
        jnp.dot(resid_low, full_query, preferred_element_type=jnp.float32) + bias_query
    ).astype(jnp.bfloat16)
    key_rows = jnp.dot(resid_low, full_key, preferred_element_type=jnp.float32).astype(jnp.bfloat16)
    value_rows = (
        jnp.dot(resid_low, full_value, preferred_element_type=jnp.float32) + bias_value
    ).astype(jnp.bfloat16)
    stacked = jnp.stack([query_rows, key_rows, value_rows], axis=1).reshape(
        item_count, slot_count, 3, model_width
    )
    head_side = lax.all_to_all(stacked, "seq", split_axis=3, concat_axis=0, tiled=True)
    mixed_heads, log_totals = lax.map(attend_forward, (head_side, group_valid))
    mixed_rows = lax.all_to_all(
        mixed_heads, "seq", split_axis=0, concat_axis=2, tiled=True
    ).reshape(token_count, model_width)
    attn_out = jnp.dot(mixed_rows, full_out, preferred_element_type=jnp.float32) + bias_out
    first_norm, first_pull = jax.vjp(layer_norm, resid + attn_out, gain_first, shift_first)
    first_low = first_norm.astype(jnp.bfloat16)
    hidden_pre = (
        jnp.einsum("td,fd->tf", first_low, full_in, preferred_element_type=jnp.float32) + bias_in
    )
    hidden, gelu_pull = jax.vjp(exact_gelu, hidden_pre)
    hidden_low = hidden.astype(jnp.bfloat16)
    ffn_out = jnp.dot(hidden_low, full_down, preferred_element_type=jnp.float32) + bias_down
    second_norm, second_pull = jax.vjp(layer_norm, first_norm + ffn_out, gain_last, shift_last)
    layer_out = (second_norm * row_keep).astype(jnp.bfloat16)
    back_query, back_key, back_value, back_out, back_in, back_down = (
        lax.all_gather(w_query, "seq", axis=0, tiled=True),
        lax.all_gather(w_key, "seq", axis=0, tiled=True),
        lax.all_gather(w_value, "seq", axis=0, tiled=True),
        lax.all_gather(w_out, "seq", axis=0, tiled=True),
        lax.all_gather(w_in, "seq", axis=0, tiled=True),
        lax.all_gather(w_down, "seq", axis=0, tiled=True),
    )
    grad_second_in, grad_gain_two, grad_shift_two = second_pull(
        cotangent.astype(jnp.float32) * row_keep
    )
    grad_ffn = grad_second_in.astype(jnp.bfloat16)
    grad_hidden = jnp.einsum("td,fd->tf", grad_ffn, back_down, preferred_element_type=jnp.float32)
    grad_pre = gelu_pull(grad_hidden)[0].astype(jnp.bfloat16)
    grad_first = grad_second_in + jnp.dot(grad_pre, back_in, preferred_element_type=jnp.float32)
    grad_first_in, grad_gain_one, grad_shift_one = first_pull(grad_first)
    grad_attn = grad_first_in.astype(jnp.bfloat16)
    grad_mixed = jnp.einsum(
        "td,ed->te", grad_attn, back_out, preferred_element_type=jnp.float32
    ).astype(jnp.bfloat16)
    grad_heads = lax.all_to_all(
        grad_mixed.reshape(item_count, slot_count, model_width),
        "seq",
        split_axis=2,
        concat_axis=0,
        tiled=True,
    )
    grad_stack = lax.map(attend_backward, (head_side, group_valid, log_totals, grad_heads))
    grad_qkv = lax.all_to_all(grad_stack, "seq", split_axis=0, concat_axis=3, tiled=True).reshape(
        token_count, 3, model_width
    )
    grad_query_rows = grad_qkv[:, 0]
    grad_key_rows = grad_qkv[:, 1]
    grad_value_rows = grad_qkv[:, 2]
    grad_resid = grad_first_in + jnp.einsum(
        "te,de->td", grad_query_rows, back_query, preferred_element_type=jnp.float32
    )
    grad_resid = grad_resid + jnp.einsum(
        "te,de->td", grad_key_rows, back_key, preferred_element_type=jnp.float32
    )
    grad_resid = grad_resid + jnp.einsum(
        "te,de->td", grad_value_rows, back_value, preferred_element_type=jnp.float32
    )
    grad_tokens = grad_resid.astype(jnp.bfloat16)
    grad_time = jnp.sum(grad_resid.reshape(item_count, slot_count, model_width), axis=1).astype(
        jnp.bfloat16
    )
    term_in = jnp.einsum("tf,td->fd", grad_pre, first_low, preferred_element_type=jnp.float32)
    term_down = jnp.einsum("tf,td->fd", hidden_low, grad_ffn, preferred_element_type=jnp.float32)
    ffn_share = lax.psum_scatter(
        jnp.concatenate([term_in, term_down], axis=1).astype(jnp.bfloat16),
        "seq",
        scatter_dimension=0,
        tiled=True,
    ).astype(jnp.float32)
    share_in = ffn_share[:, :model_width]
    share_down = ffn_share[:, model_width:]
    grad_qkv_flat = grad_qkv.reshape(token_count, 3 * model_width)
    term_qkv = jnp.einsum("tr,te->re", resid_low, grad_qkv_flat, preferred_element_type=jnp.float32)
    term_out = jnp.einsum("tr,te->re", mixed_rows, grad_attn, preferred_element_type=jnp.float32)
    term_time = jnp.einsum("tr,te->re", time_embed, grad_time, preferred_element_type=jnp.float32)
    attn_share = lax.psum_scatter(
        jnp.concatenate([term_qkv, term_out, term_time], axis=1).astype(jnp.bfloat16),
        "seq",
        scatter_dimension=0,
        tiled=True,
    ).astype(jnp.float32)
    sum_in, sum_down, sum_attn = lax.psum((share_in, share_down, attn_share), "dp")
    (
        grad_b_query,
        grad_b_value,
        grad_b_out,
        grad_b_time,
        grad_b_in,
        grad_b_down,
        sum_gain_one,
        sum_shift_one,
        sum_gain_two,
        sum_shift_two,
    ) = lax.psum(
        (
            jnp.sum(grad_query_rows, axis=0, dtype=jnp.float32),
            jnp.sum(grad_value_rows, axis=0, dtype=jnp.float32),
            jnp.sum(grad_attn, axis=0, dtype=jnp.float32),
            jnp.sum(grad_time, axis=0, dtype=jnp.float32),
            jnp.sum(grad_pre, axis=0, dtype=jnp.float32),
            jnp.sum(grad_ffn, axis=0, dtype=jnp.float32),
            grad_gain_one,
            grad_shift_one,
            grad_gain_two,
            grad_shift_two,
        ),
        ("dp", "seq"),
    )
    return (
        layer_out,
        grad_tokens,
        sum_attn[:, :model_width],
        sum_attn[:, model_width : 2 * model_width],
        sum_attn[:, 2 * model_width : 3 * model_width],
        sum_attn[:, 3 * model_width : 4 * model_width],
        sum_attn[:, 4 * model_width :],
        sum_in,
        sum_down,
        grad_b_query,
        grad_b_value,
        grad_b_out,
        grad_b_time,
        grad_b_in,
        grad_b_down,
        sum_gain_one,
        sum_shift_one,
        sum_gain_two,
        sum_shift_two,
    )


def solution(mesh):
    in_specs = (
        P(("dp", "seq"), None),
        P(("dp", "seq"), None),
        P("dp"),
        P(("dp", "seq"), None),
        P("seq", None),
        P("seq", None),
        P("seq", None),
        P("seq", None),
        P("seq", None),
        P("seq", None),
        P("seq", None),
        P(),
        P(),
        P(),
        P(),
        P(),
        P(),
        P(),
        P(),
        P(),
        P(),
    )
    out_specs = (
        P(("dp", "seq"), None),
        P(("dp", "seq"), None),
        P("seq", None),
        P("seq", None),
        P("seq", None),
        P("seq", None),
        P("seq", None),
        P("seq", None),
        P("seq", None),
        P(),
        P(),
        P(),
        P(),
        P(),
        P(),
        P(),
        P(),
        P(),
        P(),
    )
    return jax.shard_map(local, mesh=mesh, in_specs=in_specs, out_specs=out_specs, check_vma=False)
```

profile of v0, /device:TPU:0, one launch (start us, length us, event | category | flops | bytes accessed | tf_op | source)
XLA Modules:
  0.0 1024.9 jit_solution(11175937221474394372)
XLA Ops:
  11.2 23.7 %all-gather.8.cloned.1.call-done = bf16[1024,1024]{1,0:T(8,128)(2,1)} async-done(((bf16[256,1024]{1,0:T(8,128)(2,1)}), bf16[1024,1024]{1,0:T(8,128)(2,1)}) %all-gather.8.cloned.1.call-update) | async-done | bytes 2097168 | tf_op jit(solution)/shard_map/all_gather | solution.py:122
  34.9 2.0 fusion.40
  36.9 22.2 %all-gather.12.cloned.1.call-done = bf16[1024,1024]{1,0:T(8,128)(2,1)} async-done(((bf16[256,1024]{1,0:T(8,128)(2,1)}), bf16[1024,1024]{1,0:T(8,128)(2,1)}) %all-gather.12.cloned.1.call-update) | async-done | bytes 2097168 | tf_op jit(solution)/shard_map/all_gather | solution.py:119
  59.1 3.8 fusion.28
  62.9 20.3 %all-gather.10.cloned.1.call-done = bf16[1024,1024]{1,0:T(8,128)(2,1)} async-done(((bf16[256,1024]{1,0:T(8,128)(2,1)}), bf16[1024,1024]{1,0:T(8,128)(2,1)}) %all-gather.10.cloned.1.call-update) | async-done | bytes 2097168 | tf_op jit(solution)/shard_map/all_gather | solution.py:118
  83.2 3.8 fusion.30
  87.1 20.2 %all-gather.14.cloned.1.call-done = bf16[1024,1024]{1,0:T(8,128)(2,1)} async-done(((bf16[256,1024]{1,0:T(8,128)(2,1)}), bf16[1024,1024]{1,0:T(8,128)(2,1)}) %all-gather.14.cloned.1.call-update) | async-done | bytes 2097168 | tf_op jit(solution)/shard_map/all_gather | solution.py:120
  107.3 3.0 fusion.31
  110.6 5.7 copy.80
  116.3 5.1 all-to-all-start
  122.3 77.5 %all-to-all-done = bf16[1,512,3,1024]{1,2,0,3:T(4,128)(2,1)} async-done(((bf16[1,512,3,1024]{1,2,0,3:T(4,128)(2,1)}), bf16[1,512,3,1024]{1,2,0,3:T(4,128)(2,1)}, u32[]{:S(2)}, u32[]{:S(2)}) %all-to-all-start) | async-done | bytes 3145760 | tf_op jit(solution)/shard_map/all_to_all | solution.py:155
  199.8 3.0 copy.97
  202.9 16.3 %while.22 = (s32[]{:T(128)}, bf16[4,512,256]{1,2,0:T(8,128)(2,1)}, f32[4,4,512]{2,1,0:T(4,128)S(1)}, bf16[4,512,3,256]{1,3,2,0:T(8,128)(2,1)S(1)}, pred[4,512]{1,0:T(4,128)(4,1)S(1)}, /*index=5*/s32[]{:T(128)}) while((s32[]{:T(128)}, bf16[4,512,256]{1,2,0:T(8,128)(2,1)}, f32[4,4,512]{2,1,0:T(4,128)S(1)}, ...), condition=%wide.region_3.4_spmd, body=%wide.region_0.3_spmd.sunk | while | flops 281147392 | bytes 17370192 | solution.py:156
  219.2 4.3 all-to-all-start.1
  223.7 18.0 %all-to-all-done.1 = bf16[4,512,256]{1,2,0:T(8,128)(2,1)} async-done(((bf16[4,512,256]{1,2,0:T(8,128)(2,1)}), bf16[4,512,256]{1,2,0:T(8,128)(2,1)}, u32[]{:S(2)}, u32[]{:S(2)}) %all-to-all-start.1) | async-done | bytes 1048608 | tf_op jit(solution)/shard_map/all_to_all | solution.py:157
  241.7 3.6 fusion.58
  247.0 27.2 %multiply_convert_fusion.1 = (bf16[512,4096]{1,0:T(8,128)(2,1)}, f32[512,4096]{1,0:T(8,128)}, f32[512,4096]{1,0:T(8,128)}) fusion(f32[4096]{0:T(1024)S(1)} %convert_element_type.170, bf16[4096,1024]{1,0:T(8,128)(2,1)} %all-gather.18.cloned.1.call-done, f32[512,1024]{1,0:T(8,128)} %copy-done, f32[1024]{0:T(1024)S(1)} %convert_element_type.168, ...), kind=kOutput, calls=%fused_computation.37 | convolution fusion | flops 4436000768 | bytes 31485952 | tf_op jit(solution)/shard_map/td,fd->tf/dot_general | solution.py:164
  274.2 10.3 %all-gather.20.cloned.1.call-done = bf16[4096,1024]{1,0:T(8,128)(2,1)} async-done(((bf16[1024,1024]{1,0:T(8,128)(2,1)}), bf16[4096,1024]{1,0:T(8,128)(2,1)}) %all-gather.20.cloned.1.call-update) | async-done | bytes 8388624 | tf_op jit(solution)/shard_map/all_gather | solution.py:124
  284.5 10.0 fusion.59
  294.9 1.5 multiply_reduce_fusion.1
  296.4 2.0 fusion.50
  298.4 1.3 copy-done.7
  300.6 7.1 convolution_convert_fusion
  307.7 13.5 %convert_reduce_fusion = (f32[4096]{0:T(1024)S(1)}, bf16[512,4096]{1,0:T(8,128)(2,1)S(1)}) fusion(f32[512,4096]{1,0:T(8,128)} %get-tuple-element.209, f32[512,4096]{1,0:T(8,128)} %get-tuple-element.234, f32[4096]{0:T(1024)S(1)} %convert_element_type.170, bf16[512,1024]{1,0:T(8,128)(2,1)S(1)} %get-tuple-element.199, ...), kind=kOutput, calls=%fused_computation.35 | convolution fusion | flops 4330614784 | bytes 30441472 | tf_op jit(solution)/shard_map/td,fd->tf/dot_general | solution.py:183
  321.3 7.0 convolution_convert_fusion.1
  328.3 13.9 %pad_maximum_fusion = bf16[4096,2048]{0,1:T(8,128)(2,1)} fusion(bf16[4096,1024]{0,1:T(8,128)(2,1)} %convolution_convert_fusion, bf16[4096,1024]{0,1:T(8,128)(2,1)} %convolution_convert_fusion.1), kind=kLoop, calls=%fused_computation.31 | loop fusion | flops 33554432 | bytes 33554432 | tf_op jit(solution)/shard_map/concatenate | solution.py:221
  342.2 11.4 %multiply_reduce_fusion.2 = (f32[1024]{0:T(1024)S(1)}, f32[512]{0:T(512)S(1)}, f32[1024]{0:T(1024)S(1)}, f32[512,1024]{1,0:T(8,128)S(1)}) fusion(f32[512,1024]{1,0:T(8,128)} %copy-done, f32[512]{0:T(512)S(1)} %fusion.42, f32[512]{0:T(512)S(1)} %broadcast_multiply_fusion.1, f32[1024]{0:T(1024)S(1)} %convert_element_type.167, ...), kind=kOutput, calls=%fused_computation.61 | convolution fusion | flops 4300207616 | bytes 18894848 | tf_op jit(solution)/shard_map/dot_general | solution.py:185
  354.3 1.3 copy-done.5
  356.9 2.3 fusion.29
  359.2 6.2 copy.82
  365.9 9.0 reduce.7
  374.9 3.9 reshape.269
  378.8 4.3 all-to-all-start.2
  383.1 26.1 %all-to-all-done.2 = bf16[4,2,65536]{2,1,0:T(2,128)(2,1)} async-done(((bf16[4,2,65536]{2,1,0:T(2,128)(2,1)}), bf16[4,2,65536]{2,1,0:T(2,128)(2,1)}, u32[]{:S(2)}, u32[]{:S(2)}) %all-to-all-start.2) | async-done | bytes 1048608 | tf_op jit(solution)/shard_map/all_to_all | solution.py:191
  409.2 4.0 reshape.270
  413.2 2.8 copy.95
  416.1 35.0 %while.23 = (s32[]{:T(128)}, bf16[4,512,3,256]{1,3,2,0:T(8,128)(2,1)}, bf16[4,512,3,256]{1,3,2,0:T(8,128)(2,1)S(1)}, pred[4,512]{1,0:T(4,128)(4,1)S(1)}, f32[4,4...) while((s32[]{:T(128)}, bf16[4,512,3,256]{1,3,2,0:T(8,128)(2,1)}, ...), condition=%wide.region_14.15_spmd, body=%wide.region_12.14_spmd.sunk | while | flops 689829888 | bytes 39382108 | solution.py:198
  418.6 1.5 multiply_reduce_fusion.8
  420.1 1.4 multiply_convert_fusion.5
  427.4 1.5 multiply_reduce_fusion.8
  428.9 1.4 multiply_convert_fusion.5
  436.1 1.5 multiply_reduce_fusion.8
  437.6 1.4 multiply_convert_fusion.5
  444.9 1.5 multiply_reduce_fusion.8
  446.4 1.4 multiply_convert_fusion.5
  451.1 3.8 all-to-all-start.3
  455.0 4.2 convolution_convert_fusion.3
  459.2 51.5 %all-to-all-done.3 = bf16[4,512,3,256]{1,3,2,0:T(8,128)(2,1)S(1)} async-done(((bf16[4,512,3,256]{1,3,2,0:T(8,128)(2,1)}), bf16[4,512,3,256]{1,3,2,0:T(8,128)(2,1)S(1)}, u32[]{:S(2)}, u32[]{:S(2)}) %all-to-all-start.3) | async-done | bytes 3145760 | tf_op jit(solution)/shard_map/all_to_all | solution.py:199
  510.9 2.4 copy-done.35
  517.1 2.5 fusion.57
  520.0 4.0 convolution_convert_fusion.2
  524.0 9.9 pad_maximum_fusion.1
  534.0 6.8 fusion.55
  540.8 2.2 copy-done.4
  543.0 1.6 fusion.56
  544.6 1.9 copy.84
  546.5 1.8 copy.86
  548.6 41.3 %all-reduce = (f32[1024]{0:T(1024)}, f32[1024]{0:T(1024)}, f32[1024]{0:T(1024)}, f32[1024]{0:T(1024)}, f32[4096]{0:T(1024)}, /*index=5*/f32[1024]{0:T(1024)}, f3...) all-reduce(f32[1024]{0:T(1024)S(1)} %get-tuple-element.240, ...), channel_id=1, replica_groups=mesh['dp'=8,'seq'=4] {'dp','seq'}, use_global_device_ids=true, to_apply=%region_22.23 | all-reduce | flops 13312 | bytes 104448 | tf_op jit(solution)/shard_map/psum | solution.py:250
  589.9 29.4 %reduce-scatter.3.cloned.1.call-done = bf16[256,5120]{1,0:T(8,128)(2,1)} async-done(((bf16[1024,5120]{1,0:T(8,128)(2,1)}), bf16[256,5120]{1,0:T(8,128)(2,1)}) %reduce-scatter.3.cloned.1.call-update) | async-done | bytes 2621456 | tf_op jit(solution)/shard_map/reduce_scatter | solution.py:232
  619.3 267.7 %all-reduce.6 = f32[256,5120]{1,0:T(8,128)} all-reduce(bf16[256,5120]{1,0:T(8,128)(2,1)} %reduce-scatter.3.cloned.1.call-done), channel_id=1, replica_groups=mesh['dp'=8,'seq'=4] {'dp'}, use_global_device_ids=true, to_apply=%region_17.18 | all-reduce | flops 1310720 | bytes 7864320 | tf_op jit(solution)/shard_map/psum | solution.py:238
  887.0 5.0 fusion.54
  892.0 114.9 %all-reduce.5.cloned.1.call-done = (f32[1024,1024]{0,1:T(8,128)}, f32[1024,1024]{0,1:T(8,128)}) async-done(((f32[1024,1024]{0,1:T(8,128)}, f32[1024,1024]{0,1:T(8,128)}), (f32[1024,1024]{0,1:T(8,128)}, f32[1024,1024]{0,1:T(8,128)})) %all-reduce.5.cloned.1.call-update) | async-done | bytes 8388624 | tf_op jit(solution)/shard_map/psum | solution.py:238
  1006.9 5.3 copy.88
  1012.3 5.3 copy.89
  (210 shorter events, 55.0 us)
Async XLA Ops:
  7.2 4.0 copy-start.25
  7.2 4.0 copy-start.26
  7.2 27.7 %copy-start.22 = (bf16[1,1024]{1,0:T(2,128)(2,1)S(1)}, bf16[1,1024]{1,0:T(2,128)(2,1)}, u32[]{:S(2)}) copy-start(bf16[1,1024]{1,0:T(2,128)(2,1)} %param.26) | copy-start | bytes 6148
  7.2 29.7 %copy-start.27 = (bf16[1024]{0:T(1024)(128)(2,1)S(1)}, bf16[1024]{0:T(1024)(128)(2,1)}, u32[]{:S(2)}) copy-start(bf16[1024]{0:T(1024)(128)(2,1)} %param.39) | copy-start | bytes 6148
  7.2 51.9 %copy-start.12 = (bf16[512,1024]{1,0:T(8,128)(2,1)S(1)}, bf16[512,1024]{1,0:T(8,128)(2,1)}, u32[]{:S(2)}) copy-start(bf16[512,1024]{1,0:T(8,128)(2,1)} %param.25) | copy-start | bytes 3145732
  7.2 27.7 %all-gather.8.cloned.1.call-start = ((), (), s32[]{:S(2)}) async-start(), calls=%async_computation.6 | async-start | bytes 2621440 | tf_op jit(solution)/shard_map/all_gather | solution.py:122
  8.0 51.1 %all-gather.12.cloned.1.call-start = ((), (), s32[]{:S(2)}) async-start(), calls=%async_computation.8 | async-start | bytes 2621440 | tf_op jit(solution)/shard_map/all_gather | solution.py:119
  8.7 74.5 %all-gather.10.cloned.1.call-start = ((), (), s32[]{:S(2)}) async-start(), calls=%async_computation.7 | async-start | bytes 2621440 | tf_op jit(solution)/shard_map/all_gather | solution.py:118
  9.5 97.8 %all-gather.14.cloned.1.call-start = ((), (), s32[]{:S(2)}) async-start(), calls=%async_computation.9 | async-start | bytes 2621440 | tf_op jit(solution)/shard_map/all_gather | solution.py:120
  10.0 213.6 %all-gather.16.cloned.1.call-start = ((), (), s32[]{:S(2)}) async-start(), calls=%async_computation.10 | async-start | bytes 2621440 | tf_op jit(solution)/shard_map/all_gather | solution.py:121
  10.6 236.4 %all-gather.18.cloned.1.call-start = ((), (), s32[]{:S(2)}) async-start(), calls=%async_computation.11 | async-start | bytes 10485760 | tf_op jit(solution)/shard_map/all_gather | solution.py:123
  36.9 204.8 %copy-start.16 = (f32[1024]{0:T(1024)}, f32[1024]{0:T(1024)S(1)}, u32[]{:S(2)}) copy-start(f32[1024]{0:T(1024)S(1)} %convert_add_fusion.1) | copy-start | bytes 12292
  107.3 3.0 copy-start.14
  107.3 3.0 copy-start.15
  116.3 5.8 copy-start.37
  116.3 83.5 %all-to-all-start = ((bf16[1,512,3,1024]{1,2,0,3:T(4,128)(2,1)}), bf16[1,512,3,1024]{1,2,0,3:T(4,128)(2,1)}, u32[]{:S(2)}, u32[]{:S(2)}) async-start(bf16[1,512,3,1024]{1,2,0,3:T(4,128)(2,1)} %copy.80), calls=%async_computation | async-start | bytes 8388608 | tf_op jit(solution)/shard_map/all_to_all | solution.py:155
  121.4 163.1 %all-gather.20.cloned.1.call-start = ((), (), s32[]{:S(2)}) async-start(), calls=%async_computation.12 | async-start | bytes 10485760 | tf_op jit(solution)/shard_map/all_gather | solution.py:124
  202.8 20.7 %copy-start.28 = (bf16[1024]{0:T(1024)(128)(2,1)S(1)}, bf16[1024]{0:T(1024)(128)(2,1)}, u32[]{:S(2)}) copy-start(bf16[1024]{0:T(1024)(128)(2,1)} %param.38) | copy-start | bytes 6148
  202.8 20.7 %copy-start.29 = (bf16[1024]{0:T(1024)(128)(2,1)S(1)}, bf16[1024]{0:T(1024)(128)(2,1)}, u32[]{:S(2)}) copy-start(bf16[1024]{0:T(1024)(128)(2,1)} %param.42) | copy-start | bytes 6148
  202.8 20.7 %copy-start.30 = (bf16[1024]{0:T(1024)(128)(2,1)S(1)}, bf16[1024]{0:T(1024)(128)(2,1)}, u32[]{:S(2)}) copy-start(bf16[1024]{0:T(1024)(128)(2,1)} %param.43) | copy-start | bytes 6148
  202.8 20.7 %copy-start.24 = (bf16[4096]{0:T(1024)(128)(2,1)S(1)}, bf16[4096]{0:T(1024)(128)(2,1)}, u32[]{:S(2)}) copy-start(bf16[4096]{0:T(1024)(128)(2,1)} %param.40) | copy-start | bytes 24580
  202.8 20.7 %copy-start.31 = (bf16[1024]{0:T(1024)(128)(2,1)S(1)}, bf16[1024]{0:T(1024)(128)(2,1)}, u32[]{:S(2)}) copy-start(bf16[1024]{0:T(1024)(128)(2,1)} %param.41) | copy-start | bytes 6148
  202.9 20.7 %copy-start.32 = (bf16[1024]{0:T(1024)(128)(2,1)S(1)}, bf16[1024]{0:T(1024)(128)(2,1)}, u32[]{:S(2)}) copy-start(bf16[1024]{0:T(1024)(128)(2,1)} %param.44) | copy-start | bytes 6148
  202.9 20.7 %copy-start.33 = (bf16[1024]{0:T(1024)(128)(2,1)S(1)}, bf16[1024]{0:T(1024)(128)(2,1)}, u32[]{:S(2)}) copy-start(bf16[1024]{0:T(1024)(128)(2,1)} %param.45) | copy-start | bytes 6148
  219.2 4.3 copy-start.18
  219.2 22.5 %all-to-all-start.1 = ((bf16[4,512,256]{1,2,0:T(8,128)(2,1)}), bf16[4,512,256]{1,2,0:T(8,128)(2,1)}, u32[]{:S(2)}, u32[]{:S(2)}) async-start(bf16[4,512,256]{1,2,0:T(8,128)(2,1)} %get-tuple-element.79), calls=%async_computation.1 | async-start | bytes 2097152 | tf_op jit(solution)/shard_map/all_to_all | solution.py:157
  223.4 310.5 %reduce-scatter.5.cloned.1.call-start = ((), (), s32[]{:S(2)}) async-start(), calls=%async_computation.14 | async-start | bytes 20971520 | tf_op jit(solution)/shard_map/reduce_scatter | solution.py:220
  245.3 1.3 copy-start
  284.5 10.3 %copy-start.8 = (bf16[512,1024]{1,0:T(8,128)(2,1)S(1)}, bf16[512,1024]{1,0:T(8,128)(2,1)}, u32[]{:S(2)}) copy-start(bf16[512,1024]{1,0:T(8,128)(2,1)} %param.28) | copy-start | bytes 3145732
  296.4 4.2 copy-start.38
  298.4 1.3 copy-start.7
  307.7 13.5 %copy-start.1 = (f32[512,1024]{1,0:T(8,128)S(1)}, f32[512,1024]{1,0:T(8,128)}, u32[]{:S(2)}) copy-start(f32[512,1024]{1,0:T(8,128)} %copy-done) | copy-start | bytes 6291460
  321.2 7.0 copy-start.39
  342.2 11.4 %copy-start.2 = (f32[512,1024]{1,0:T(8,128)S(1)}, f32[512,1024]{1,0:T(8,128)}, u32[]{:S(2)}) copy-start(f32[512,1024]{1,0:T(8,128)} %copy-done) | copy-start | bytes 6291460
  353.6 3.3 copy-start.10
  354.3 1.3 copy-start.5
  355.9 1.0 copy-start.11
  378.8 30.4 %all-to-all-start.2 = ((bf16[4,2,65536]{2,1,0:T(2,128)(2,1)}), bf16[4,2,65536]{2,1,0:T(2,128)(2,1)}, u32[]{:S(2)}, u32[]{:S(2)}) async-start(bf16[4,2,65536]{2,1,0:T(2,128)(2,1)} %reshape.269), calls=%async_computation.2 | async-start | bytes 2097152 | tf_op jit(solution)/shard_map/all_to_all | solution.py:191
  451.1 3.9 copy-start.23
  451.1 59.6 %all-to-all-start.3 = ((bf16[4,512,3,256]{1,3,2,0:T(8,128)(2,1)}), bf16[4,512,3,256]{1,3,2,0:T(8,128)(2,1)S(1)}, u32[]{:S(2)}, u32[]{:S(2)}) async-start(bf16[4,512,3,256]{1,3,2,0:T(8,128)(2,1)} %get-tuple-element.81), calls=%async_computation.3 | async-start | bytes 6291456 | tf_op jit(solution)/shard_map/all_to_all | solution.py:199
  454.9 164.4 %reduce-scatter.3.cloned.1.call-start = ((), (), s32[]{:S(2)}) async-start(), calls=%async_computation.13 | async-start | bytes 13107200 | tf_op jit(solution)/shard_map/reduce_scatter | solution.py:232
  510.6 2.6 copy-start.35
  510.9 9.1 copy-start.3
  513.3 1.6 copy-start.34
  514.8 1.6 copy-start.6
  514.9 2.2 copy-start.36
  517.1 2.9 copy-start.13
  517.1 2.9 copy-start.17
  520.0 4.0 copy-start.9
  533.9 473.0 %all-reduce.5.cloned.1.call-start = ((), (), s32[]{:S(2)}) async-start(), calls=%async_computation.15 | async-start | bytes 16777216 | tf_op jit(solution)/shard_map/psum | solution.py:238
  540.8 2.3 copy-start.4
  544.6 4.0 copy-start.19
  544.6 4.0 copy-start.20
  544.6 4.0 copy-start.21
Sparse Core Ops, SparseCore 0:
  9.6 25.2 all-gather.7
  36.5 22.5 all-gather.11
  60.7 22.5 all-gather.9
  84.7 22.5 all-gather.13
  108.7 27.7 all-gather.15
  137.9 83.4 all-gather.17
  223.0 61.5 all-gather.19
  342.3 155.0 reduce-scatter.4
  534.0 85.2 reduce-scatter.2
  624.4 382.4 all-reduce.4
where the time goes:
time: 1030 us; the launch traced here: 1020 us
  waiting for transfers between devices  419 us (41%)
  blocking collectives  309 us (30%)
  matrix products  135 us (13%)
  local copies, waits for them, and re-layouts  75.6 us (7%)
  other arithmetic  52.9 us (5%)
  starting transfers between devices  17.8 us (2%)
  between operations  15.3 us (1%)
    psum x1, blocking collectives, local(): lax.psum((share_in, share_down, attn_share), 'dp')  268 us
    psum x1, waiting for transfers between devices, local(): lax.psum((share_in, share_down, attn_share), 'dp')  115 us
    all_to_all x1, waiting for transfers between devices, local(): lax.all_to_all(stacked, 'seq', split_axis=3, concat_axis=0, tiled=True)  77.5 us
    all_to_all x1, waiting for transfers between devices, local(): lax.all_to_all(grad_stack, 'seq', split_axis=0, concat_axis=3, tiled=True)  51.5 us
    psum x1, blocking collectives, local(): lax.psum((jnp.sum(grad_query_rows, axis=0, dtype=jnp.float32), jnp.sum(gr...  41.3 us
    unnamed x86, local copies, waits for them, and re-layouts  32.8 us
    reduce_scatter x1, waiting for transfers between devices, local(): lax.psum_scatter(jnp.concatenate([term_qkv, term_out, term_time], axis=1)...  29.4 us
    dot_general x1, matrix products, local(): jnp.einsum('td,fd->tf', first_low, full_in, preferred_element_type=jnp.fl...  27.2 us
  transfers between devices with their start and end apart: 14, of which 11 were waited for; matrix products, arithmetic and copies ran while one was open for 18% of the time, Pallas kernels for 0%

commit v1 on v0

--- a/solution.py
+++ b/solution.py
@@ -1,3 +1,4 @@
+import functools
 import jax
 import jax.numpy as jnp
 from jax import lax
@@ -7,6 +8,18 @@
 BLOCK = 25
 norm_eps = 1e-05
 neg_large = -1e30
+
+
+def begin_object(chunk, mesh_dim):
+    return jnp.concatenate(
+        lax.all_to_all(
+            jnp.stack(jnp.split(chunk, lax.axis_size(mesh_dim), axis=3)), mesh_dim, 0, 0
+        ),
+        axis=0,
+    )
+
+
+circles_serve = functools.partial(begin_object, mesh_dim="seq")
 
 
 def layer_norm(values, gain, shift):
@@ -152,7 +165,7 @@
     stacked = jnp.stack([query_rows, key_rows, value_rows], axis=1).reshape(
         item_count, slot_count, 3, model_width
     )
-    head_side = lax.all_to_all(stacked, "seq", split_axis=3, concat_axis=0, tiled=True)
+    head_side = circles_serve(stacked)
     mixed_heads, log_totals = lax.map(attend_forward, (head_side, group_valid))
     mixed_rows = lax.all_to_all(
         mixed_heads, "seq", split_axis=0, concat_axis=2, tiled=True

time: 1030 us -> 1030 us (level)
    all_to_all x1, waiting for transfers between devices: 77.5 us -> 54.8 us  [begin_object(): lax.all_to_all(jnp.stack(jnp.split(chunk, lax.axis_size(mesh_dim), axis=3...]
    all_gather x1, waiting for transfers between devices: 10.3 us -> 24.9 us  [local(): lax.all_gather(w_down, 'seq', axis=0, tiled=True)]
    unnamed x86 -> x84, local copies, waits for them, and re-layouts: 32.8 us -> 35.1 us
where the time goes in v1:
time: 1030 us; the launch traced here: 1020 us
  waiting for transfers between devices  415 us (40%)
  blocking collectives  309 us (30%)
  matrix products  134 us (13%)
  local copies, waits for them, and re-layouts  72.7 us (7%)
  other arithmetic  54.8 us (5%)
  starting transfers between devices  16.6 us (2%)
  between operations  15.3 us (1%)
    psum x1, blocking collectives, local(): lax.psum((share_in, share_down, attn_share), 'dp')  268 us
    psum x1, waiting for transfers between devices, local(): lax.psum((share_in, share_down, attn_share), 'dp')  115 us
    all_to_all x1, waiting for transfers between devices, begin_object(): lax.all_to_all(jnp.stack(jnp.split(chunk, lax.axis_size(mesh_dim), axis=3...  54.8 us
    all_to_all x1, waiting for transfers between devices, local(): lax.all_to_all(grad_stack, 'seq', split_axis=0, concat_axis=3, tiled=True)  50.7 us
    psum x1, blocking collectives, local(): lax.psum((jnp.sum(grad_query_rows, axis=0, dtype=jnp.float32), jnp.sum(gr...  41.3 us
    unnamed x84, local copies, waits for them, and re-layouts  35.1 us
    reduce_scatter x1, waiting for transfers between devices, local(): lax.psum_scatter(jnp.concatenate([term_qkv, term_out, term_time], axis=1)...  29.4 us
    dot_general x1, matrix products, local(): jnp.einsum('td,fd->tf', first_low, full_in, preferred_element_type=jnp.fl...  27.7 us
  transfers between devices with their start and end apart: 14, of which 11 were waited for; matrix products, arithmetic and copies ran while one was open for 18% of the time, Pallas kernels for 0%

profile of v1, /device:TPU:0, one launch (start us, length us, event | category | flops | bytes accessed | tf_op | source)
XLA Modules:
  0.0 1017.9 jit_solution(3835326753239374456)
XLA Ops:
  11.2 23.7 %all-gather.8.cloned.1.call-done = bf16[1024,1024]{1,0:T(8,128)(2,1)} async-done(((bf16[256,1024]{1,0:T(8,128)(2,1)}), bf16[1024,1024]{1,0:T(8,128)(2,1)}) %all-gather.8.cloned.1.call-update) | async-done | bytes 2097168 | tf_op jit(solution)/shard_map/all_gather | solution.py:135
  34.9 2.0 fusion.40
  36.9 22.2 %all-gather.12.cloned.1.call-done = bf16[1024,1024]{1,0:T(8,128)(2,1)} async-done(((bf16[256,1024]{1,0:T(8,128)(2,1)}), bf16[1024,1024]{1,0:T(8,128)(2,1)}) %all-gather.12.cloned.1.call-update) | async-done | bytes 2097168 | tf_op jit(solution)/shard_map/all_gather | solution.py:132
  59.1 2.8 fusion.28
  61.9 21.3 %all-gather.10.cloned.1.call-done = bf16[1024,1024]{1,0:T(8,128)(2,1)} async-done(((bf16[256,1024]{1,0:T(8,128)(2,1)}), bf16[1024,1024]{1,0:T(8,128)(2,1)}) %all-gather.10.cloned.1.call-update) | async-done | bytes 2097168 | tf_op jit(solution)/shard_map/all_gather | solution.py:131
  83.2 2.8 fusion.30
  86.1 21.2 %all-gather.14.cloned.1.call-done = bf16[1024,1024]{1,0:T(8,128)(2,1)} async-done(((bf16[256,1024]{1,0:T(8,128)(2,1)}), bf16[1024,1024]{1,0:T(8,128)(2,1)}) %all-gather.14.cloned.1.call-update) | async-done | bytes 2097168 | tf_op jit(solution)/shard_map/all_gather | solution.py:133
  107.2 2.8 fusion.31
  110.7 1.9 pad_maximum_fusion.2
  112.6 3.9 all-to-all-start
  117.4 54.8 %all-to-all-done = bf16[4,1,512,3,256]{4,2,3,1,0:T(8,128)(2,1)S(1)} async-done(((bf16[4,1,512,3,256]{4,2,3,1,0:T(8,128)(2,1)}), bf16[4,1,512,3,256]{4,2,3,1,0:T(8,128)(2,1)S(1)}, u32[]{:S(2)}, u32[]{:S(2)}) %all-to-all-start) | async-done | bytes 3145760 | tf_op jit(solution)/shard_map/all_to_all | solution.py:15
  172.2 1.7 copy-done.3
  173.9 3.2 copy.82
  177.1 16.3 %while.22 = (s32[]{:T(128)}, bf16[4,512,256]{1,2,0:T(8,128)(2,1)}, f32[4,4,512]{2,1,0:T(4,128)S(1)}, bf16[4,512,3,256]{1,3,2,0:T(8,128)(2,1)S(1)}, pred[4,512]{1,0:T(4,128)(4,1)S(1)}, /*index=5*/s32[]{:T(128)}) while((s32[]{:T(128)}, bf16[4,512,256]{1,2,0:T(8,128)(2,1)}, f32[4,4,512]{2,1,0:T(4,128)S(1)}, ...), condition=%wide.region_3.4_spmd, body=%wide.region_0.3_spmd.sunk | while | flops 281147392 | bytes 17370192 | solution.py:169
  193.4 4.3 all-to-all-start.1
  197.9 21.8 %all-to-all-done.1 = bf16[4,512,256]{1,2,0:T(8,128)(2,1)} async-done(((bf16[4,512,256]{1,2,0:T(8,128)(2,1)}), bf16[4,512,256]{1,2,0:T(8,128)(2,1)}, u32[]{:S(2)}, u32[]{:S(2)}) %all-to-all-start.1) | async-done | bytes 1048608 | tf_op jit(solution)/shard_map/all_to_all | solution.py:170
  219.7 3.6 fusion.58
  225.0 27.7 %multiply_convert_fusion.1 = (bf16[512,4096]{1,0:T(8,128)(2,1)}, f32[512,4096]{1,0:T(8,128)}, f32[512,4096]{1,0:T(8,128)}) fusion(f32[4096]{0:T(1024)S(1)} %convert_element_type.170, bf16[4096,1024]{1,0:T(8,128)(2,1)} %all-gather.18.cloned.1.call-done, f32[512,1024]{1,0:T(8,128)} %copy-done, f32[1024]{0:T(1024)S(1)} %convert_element_type.168, ...), kind=kOutput, calls=%fused_computation.37 | convolution fusion | flops 4436000768 | bytes 31485952 | tf_op jit(solution)/shard_map/td,fd->tf/dot_general | solution.py:177
  252.7 24.9 %all-gather.20.cloned.1.call-done = bf16[4096,1024]{1,0:T(8,128)(2,1)} async-done(((bf16[1024,1024]{1,0:T(8,128)(2,1)}), bf16[4096,1024]{1,0:T(8,128)(2,1)}) %all-gather.20.cloned.1.call-update) | async-done | bytes 8388624 | tf_op jit(solution)/shard_map/all_gather | solution.py:137
  277.6 10.0 fusion.59
  287.9 1.5 multiply_reduce_fusion.1
  289.4 2.0 fusion.50
  291.4 1.3 copy-done.8
  293.6 7.1 convolution_convert_fusion
  300.7 13.5 %convert_reduce_fusion = (f32[4096]{0:T(1024)S(1)}, bf16[512,4096]{1,0:T(8,128)(2,1)S(1)}) fusion(f32[512,4096]{1,0:T(8,128)} %get-tuple-element.253, f32[512,4096]{1,0:T(8,128)} %get-tuple-element.282, f32[4096]{0:T(1024)S(1)} %convert_element_type.170, bf16[512,1024]{1,0:T(8,128)(2,1)S(1)} %get-tuple-element.243, ...), kind=kOutput, calls=%fused_computation.35 | convolution fusion | flops 4330614784 | bytes 30441472 | tf_op jit(solution)/shard_map/td,fd->tf/dot_general | solution.py:196
  314.3 7.0 convolution_convert_fusion.1
  321.3 13.9 %pad_maximum_fusion = bf16[4096,2048]{0,1:T(8,128)(2,1)} fusion(bf16[4096,1024]{0,1:T(8,128)(2,1)} %convolution_convert_fusion, bf16[4096,1024]{0,1:T(8,128)(2,1)} %convolution_convert_fusion.1), kind=kLoop, calls=%fused_computation.31 | loop fusion | flops 33554432 | bytes 33554432 | tf_op jit(solution)/shard_map/concatenate | solution.py:234
  335.3 11.4 %multiply_reduce_fusion.2 = (f32[1024]{0:T(1024)S(1)}, f32[512]{0:T(512)S(1)}, f32[1024]{0:T(1024)S(1)}, f32[512,1024]{1,0:T(8,128)S(1)}) fusion(f32[512,1024]{1,0:T(8,128)} %copy-done, f32[512]{0:T(512)S(1)} %fusion.42, f32[512]{0:T(512)S(1)} %broadcast_multiply_fusion.1, f32[1024]{0:T(1024)S(1)} %convert_element_type.167, ...), kind=kOutput, calls=%fused_computation.61 | convolution fusion | flops 4300207616 | bytes 18894848 | tf_op jit(solution)/shard_map/dot_general | solution.py:198
  350.6 2.3 fusion.29
  352.9 6.2 copy.83
  359.6 9.0 reduce.7
  368.6 3.9 reshape.273
  372.5 4.3 all-to-all-start.2
  376.8 26.1 %all-to-all-done.2 = bf16[4,2,65536]{2,1,0:T(2,128)(2,1)} async-done(((bf16[4,2,65536]{2,1,0:T(2,128)(2,1)}), bf16[4,2,65536]{2,1,0:T(2,128)(2,1)}, u32[]{:S(2)}, u32[]{:S(2)}) %all-to-all-start.2) | async-done | bytes 1048608 | tf_op jit(solution)/shard_map/all_to_all | solution.py:204
  402.9 4.0 reshape.274
  406.9 2.8 copy.97
  409.7 35.0 %while.23 = (s32[]{:T(128)}, bf16[4,512,3,256]{1,3,2,0:T(8,128)(2,1)}, bf16[4,512,3,256]{1,3,2,0:T(8,128)(2,1)S(1)}, pred[4,512]{1,0:T(4,128)(4,1)S(1)}, f32[4,4...) while((s32[]{:T(128)}, bf16[4,512,3,256]{1,3,2,0:T(8,128)(2,1)}, ...), condition=%wide.region_14.15_spmd, body=%wide.region_12.14_spmd.sunk | while | flops 689829888 | bytes 39382108 | solution.py:211
  412.3 1.5 multiply_reduce_fusion.8
  413.8 1.4 multiply_convert_fusion.5
  421.1 1.5 multiply_reduce_fusion.8
  422.6 1.4 multiply_convert_fusion.5
  429.8 1.5 multiply_reduce_fusion.8
  431.3 1.4 multiply_convert_fusion.5
  438.6 1.5 multiply_reduce_fusion.8
  440.1 1.4 multiply_convert_fusion.5
  444.8 3.8 all-to-all-start.3
  448.7 4.3 convolution_convert_fusion.3
  453.0 50.7 %all-to-all-done.3 = bf16[4,512,3,256]{1,3,2,0:T(8,128)(2,1)S(1)} async-done(((bf16[4,512,3,256]{1,3,2,0:T(8,128)(2,1)}), bf16[4,512,3,256]{1,3,2,0:T(8,128)(2,1)S(1)}, u32[]{:S(2)}, u32[]{:S(2)}) %all-to-all-start.3) | async-done | bytes 3145760 | tf_op jit(solution)/shard_map/all_to_all | solution.py:212
  503.9 2.4 copy-done.34
  510.1 2.5 fusion.57
  513.0 4.0 convolution_convert_fusion.2
  517.0 9.9 pad_maximum_fusion.1
  527.0 6.8 fusion.55
  533.8 2.2 copy-done.5
  536.0 1.6 fusion.56
  537.6 1.9 copy.86
  539.5 1.8 copy.88
  541.6 41.3 %all-reduce = (f32[1024]{0:T(1024)}, f32[1024]{0:T(1024)}, f32[1024]{0:T(1024)}, f32[1024]{0:T(1024)}, f32[4096]{0:T(1024)}, /*index=5*/f32[1024]{0:T(1024)}, f3...) all-reduce(f32[1024]{0:T(1024)S(1)} %get-tuple-element.288, ...), channel_id=1, replica_groups=mesh['dp'=8,'seq'=4] {'dp','seq'}, use_global_device_ids=true, to_apply=%region_22.23 | all-reduce | flops 13312 | bytes 104448 | tf_op jit(solution)/shard_map/psum | solution.py:263
  583.0 29.4 %reduce-scatter.3.cloned.1.call-done = bf16[256,5120]{1,0:T(8,128)(2,1)} async-done(((bf16[1024,5120]{1,0:T(8,128)(2,1)}), bf16[256,5120]{1,0:T(8,128)(2,1)}) %reduce-scatter.3.cloned.1.call-update) | async-done | bytes 2621456 | tf_op jit(solution)/shard_map/reduce_scatter | solution.py:245
  612.3 267.6 %all-reduce.6 = f32[256,5120]{1,0:T(8,128)} all-reduce(bf16[256,5120]{1,0:T(8,128)(2,1)} %reduce-scatter.3.cloned.1.call-done), channel_id=1, replica_groups=mesh['dp'=8,'seq'=4] {'dp'}, use_global_device_ids=true, to_apply=%region_17.18 | all-reduce | flops 1310720 | bytes 7864320 | tf_op jit(solution)/shard_map/psum | solution.py:251
  880.0 5.0 fusion.54
  885.0 114.9 %all-reduce.5.cloned.1.call-done = (f32[1024,1024]{0,1:T(8,128)}, f32[1024,1024]{0,1:T(8,128)}) async-done(((f32[1024,1024]{0,1:T(8,128)}, f32[1024,1024]{0,1:T(8,128)}), (f32[1024,1024]{0,1:T(8,128)}, f32[1024,1024]{0,1:T(8,128)})) %all-reduce.5.cloned.1.call-update) | async-done | bytes 8388624 | tf_op jit(solution)/shard_map/psum | solution.py:251
  999.9 5.3 copy.90
  1005.2 5.3 copy.91
  (209 shorter events, 57.2 us)
Async XLA Ops:
  7.2 4.0 copy-start.24
  7.2 4.0 copy-start.25
  7.2 27.7 %copy-start.21 = (bf16[1,1024]{1,0:T(2,128)(2,1)S(1)}, bf16[1,1024]{1,0:T(2,128)(2,1)}, u32[]{:S(2)}) copy-start(bf16[1,1024]{1,0:T(2,128)(2,1)} %param.26) | copy-start | bytes 6148
  7.2 27.7 %all-gather.8.cloned.1.call-start = ((), (), s32[]{:S(2)}) async-start(), calls=%async_computation.6 | async-start | bytes 2621440 | tf_op jit(solution)/shard_map/all_gather | solution.py:135
  8.0 28.9 %copy-start.26 = (bf16[1024]{0:T(1024)(128)(2,1)S(1)}, bf16[1024]{0:T(1024)(128)(2,1)}, u32[]{:S(2)}) copy-start(bf16[1024]{0:T(1024)(128)(2,1)} %param.39) | copy-start | bytes 6148
  8.0 51.1 %copy-start.13 = (bf16[512,1024]{1,0:T(8,128)(2,1)S(1)}, bf16[512,1024]{1,0:T(8,128)(2,1)}, u32[]{:S(2)}) copy-start(bf16[512,1024]{1,0:T(8,128)(2,1)} %param.25) | copy-start | bytes 3145732
  8.0 51.1 %all-gather.12.cloned.1.call-start = ((), (), s32[]{:S(2)}) async-start(), calls=%async_computation.8 | async-start | bytes 2621440 | tf_op jit(solution)/shard_map/all_gather | solution.py:132
  8.7 74.5 %all-gather.10.cloned.1.call-start = ((), (), s32[]{:S(2)}) async-start(), calls=%async_computation.7 | async-start | bytes 2621440 | tf_op jit(solution)/shard_map/all_gather | solution.py:131
  9.5 97.8 %all-gather.14.cloned.1.call-start = ((), (), s32[]{:S(2)}) async-start(), calls=%async_computation.9 | async-start | bytes 2621440 | tf_op jit(solution)/shard_map/all_gather | solution.py:133
  10.0 187.9 %all-gather.16.cloned.1.call-start = ((), (), s32[]{:S(2)}) async-start(), calls=%async_computation.10 | async-start | bytes 2621440 | tf_op jit(solution)/shard_map/all_gather | solution.py:134
  10.6 214.3 %all-gather.18.cloned.1.call-start = ((), (), s32[]{:S(2)}) async-start(), calls=%async_computation.11 | async-start | bytes 10485760 | tf_op jit(solution)/shard_map/all_gather | solution.py:136
  36.9 182.8 %copy-start.15 = (f32[1024]{0:T(1024)}, f32[1024]{0:T(1024)S(1)}, u32[]{:S(2)}) copy-start(f32[1024]{0:T(1024)S(1)} %convert_add_fusion.1) | copy-start | bytes 12292
  112.6 4.7 copy-start.36
  112.6 59.6 %all-to-all-start = ((bf16[4,1,512,3,256]{4,2,3,1,0:T(8,128)(2,1)}), bf16[4,1,512,3,256]{4,2,3,1,0:T(8,128)(2,1)S(1)}, u32[]{:S(2)}, u32[]{:S(2)}) async-start(bf16[4,1,512,3,256]{4,2,3,1,0:T(8,128)(2,1)} %pad_maximum_fusion.2), calls=%async_computation | async-start | bytes 6291456 | tf_op jit(solution)/shard_map/all_to_all | solution.py:15
  116.5 161.0 %all-gather.20.cloned.1.call-start = ((), (), s32[]{:S(2)}) async-start(), calls=%async_computation.12 | async-start | bytes 10485760 | tf_op jit(solution)/shard_map/all_gather | solution.py:137
  172.2 1.7 copy-start.3
  177.1 20.7 %copy-start.27 = (bf16[1024]{0:T(1024)(128)(2,1)S(1)}, bf16[1024]{0:T(1024)(128)(2,1)}, u32[]{:S(2)}) copy-start(bf16[1024]{0:T(1024)(128)(2,1)} %param.38) | copy-start | bytes 6148
  177.1 20.7 %copy-start.28 = (bf16[1024]{0:T(1024)(128)(2,1)S(1)}, bf16[1024]{0:T(1024)(128)(2,1)}, u32[]{:S(2)}) copy-start(bf16[1024]{0:T(1024)(128)(2,1)} %param.42) | copy-start | bytes 6148
  177.1 20.7 %copy-start.29 = (bf16[1024]{0:T(1024)(128)(2,1)S(1)}, bf16[1024]{0:T(1024)(128)(2,1)}, u32[]{:S(2)}) copy-start(bf16[1024]{0:T(1024)(128)(2,1)} %param.43) | copy-start | bytes 6148
  177.1 20.7 %copy-start.23 = (bf16[4096]{0:T(1024)(128)(2,1)S(1)}, bf16[4096]{0:T(1024)(128)(2,1)}, u32[]{:S(2)}) copy-start(bf16[4096]{0:T(1024)(128)(2,1)} %param.40) | copy-start | bytes 24580
  177.1 20.7 %copy-start.30 = (bf16[1024]{0:T(1024)(128)(2,1)S(1)}, bf16[1024]{0:T(1024)(128)(2,1)}, u32[]{:S(2)}) copy-start(bf16[1024]{0:T(1024)(128)(2,1)} %param.41) | copy-start | bytes 6148
  177.1 20.7 %copy-start.31 = (bf16[1024]{0:T(1024)(128)(2,1)S(1)}, bf16[1024]{0:T(1024)(128)(2,1)}, u32[]{:S(2)}) copy-start(bf16[1024]{0:T(1024)(128)(2,1)} %param.44) | copy-start | bytes 6148
  177.1 20.8 %copy-start.32 = (bf16[1024]{0:T(1024)(128)(2,1)S(1)}, bf16[1024]{0:T(1024)(128)(2,1)}, u32[]{:S(2)}) copy-start(bf16[1024]{0:T(1024)(128)(2,1)} %param.45) | copy-start | bytes 6148
  193.4 4.3 copy-start.17
  193.4 26.3 %all-to-all-start.1 = ((bf16[4,512,256]{1,2,0:T(8,128)(2,1)}), bf16[4,512,256]{1,2,0:T(8,128)(2,1)}, u32[]{:S(2)}, u32[]{:S(2)}) async-start(bf16[4,512,256]{1,2,0:T(8,128)(2,1)} %get-tuple-element.79), calls=%async_computation.1 | async-start | bytes 2097152 | tf_op jit(solution)/shard_map/all_to_all | solution.py:170
  197.7 329.3 %reduce-scatter.5.cloned.1.call-start = ((), (), s32[]{:S(2)}) async-start(), calls=%async_computation.14 | async-start | bytes 20971520 | tf_op jit(solution)/shard_map/reduce_scatter | solution.py:233
  223.3 1.3 copy-start
  277.6 10.3 %copy-start.9 = (bf16[512,1024]{1,0:T(8,128)(2,1)S(1)}, bf16[512,1024]{1,0:T(8,128)(2,1)}, u32[]{:S(2)}) copy-start(bf16[512,1024]{1,0:T(8,128)(2,1)} %param.28) | copy-start | bytes 3145732
  289.4 4.2 copy-start.37
  291.4 1.3 copy-start.8
  300.7 13.6 %copy-start.1 = (f32[512,1024]{1,0:T(8,128)S(1)}, f32[512,1024]{1,0:T(8,128)}, u32[]{:S(2)}) copy-start(f32[512,1024]{1,0:T(8,128)} %copy-done) | copy-start | bytes 6291460
  314.3 7.0 copy-start.38
  335.2 11.5 %copy-start.2 = (f32[512,1024]{1,0:T(8,128)S(1)}, f32[512,1024]{1,0:T(8,128)}, u32[]{:S(2)}) copy-start(f32[512,1024]{1,0:T(8,128)} %copy-done) | copy-start | bytes 6291460
  347.4 1.3 copy-start.6
  347.4 3.2 copy-start.11
  349.0 1.0 copy-start.12
  372.5 30.4 %all-to-all-start.2 = ((bf16[4,2,65536]{2,1,0:T(2,128)(2,1)}), bf16[4,2,65536]{2,1,0:T(2,128)(2,1)}, u32[]{:S(2)}, u32[]{:S(2)}) async-start(bf16[4,2,65536]{2,1,0:T(2,128)(2,1)} %reshape.273), calls=%async_computation.2 | async-start | bytes 2097152 | tf_op jit(solution)/shard_map/all_to_all | solution.py:204
  444.8 3.9 copy-start.22
  444.8 58.9 %all-to-all-start.3 = ((bf16[4,512,3,256]{1,3,2,0:T(8,128)(2,1)}), bf16[4,512,3,256]{1,3,2,0:T(8,128)(2,1)S(1)}, u32[]{:S(2)}, u32[]{:S(2)}) async-start(bf16[4,512,3,256]{1,3,2,0:T(8,128)(2,1)} %get-tuple-element.81), calls=%async_computation.3 | async-start | bytes 6291456 | tf_op jit(solution)/shard_map/all_to_all | solution.py:212
  448.6 163.7 %reduce-scatter.3.cloned.1.call-start = ((), (), s32[]{:S(2)}) async-start(), calls=%async_computation.13 | async-start | bytes 13107200 | tf_op jit(solution)/shard_map/reduce_scatter | solution.py:245
  503.7 2.6 copy-start.34
  503.9 9.1 copy-start.4
  506.3 1.6 copy-start.33
  507.9 1.6 copy-start.7
  507.9 2.2 copy-start.35
  510.1 2.9 copy-start.14
  510.1 2.9 copy-start.16
  513.0 4.0 copy-start.10
  526.9 473.0 %all-reduce.5.cloned.1.call-start = ((), (), s32[]{:S(2)}) async-start(), calls=%async_computation.15 | async-start | bytes 16777216 | tf_op jit(solution)/shard_map/psum | solution.py:251
  533.8 2.3 copy-start.5
  537.6 4.0 copy-start.18
  537.6 4.0 copy-start.19
  537.6 4.0 copy-start.20
Sparse Core Ops, SparseCore 0:
  9.6 25.2 all-gather.7
  36.5 22.5 all-gather.11
  60.6 22.5 all-gather.9
  84.6 22.5 all-gather.13
  108.6 32.7 all-gather.15
  142.9 74.5 all-gather.17
  219.0 58.5 all-gather.19
  335.4 154.3 reduce-scatter.4
  527.0 85.2 reduce-scatter.2
  617.4 382.4 all-reduce.4
